TPU v7x, 128 devices: a whole 4x4x4 slice. The times are simulated.
128 devices in a mesh: section: 4 (over z_lo, core), dp: 8 (over x, z_hi), mp: 4 (over y).
Axes of the slice: x: 4, y: 4, z: 4 (z_hi: 2, z_lo: 2; z = z_hi * 2 + z_lo), core: 2. Of those that a mesh axis runs over, the one named last changes fastest.
Arguments:
- entrance: bfloat16 [8, 2, 96, 4096], P('dp'), may hold values from -6 to 6
- lengths: int32 [8, 2], P('dp'), may hold values from 24 to 96
- positives: int32 [8], replicated, may hold values from 0 to 7, each once
- norm_gains: float32 [4, 4096], P('section'), may hold values from 0.5 to 1.5
- query_proj: bfloat16 [4, 4096, 2048], P('section', None, 'mp'), may hold values from -0.09375 to 0.09375
- key_proj: bfloat16 [4, 4096, 512], P('section', None, 'mp'), may hold values from -0.09375 to 0.09375
- value_proj: bfloat16 [4, 4096, 512], P('section', None, 'mp'), may hold values from -0.09375 to 0.09375
- out_proj: bfloat16 [4, 2048, 4096], P('section', 'mp'), may hold values from -0.125 to 0.125
Outputs:
- losses: float32 [4, 7], P('section')
- norm_gain_grad: float32 [4, 4096], P('section', ('dp', 'mp'))
- query_proj_grad: float32 [4, 4096, 2048], P('section', 'dp', 'mp')
- key_proj_grad: float32 [4, 4096, 512], P('section', 'dp', 'mp')
- value_proj_grad: float32 [4, 4096, 512], P('section', 'dp', 'mp')
- out_proj_grad: float32 [4, 2048, 4096], P('section', 'mp', 'dp')
Inputs may be any that keep to these rules, and one draw needn't show every extreme that they name: positives is a permutation of the pair indices. `lengths`: tokens at or past a sequence's length are padding.
All inputs are finite; a program needn't handle non-finite values.
Results may differ from a plain program's by a relative error of at most 0.039.
Values may be sent and summed in bfloat16 or wider, within the bound.
No kernel may reach another device: no remote copies, remote signals or barrier semaphores. Data moves between devices by JAX's collectives and lax.ppermute only.
A program may use at most 128 MiB of HBM per device.

v0:
```python
import jax
import jax.numpy as jnp
from jax import lax
from jax.sharding import PartitionSpec as P

HEAD = 128
WIDTHS = 7
EPSILON = 1e-05
SOFTMAX_TEMPER = 0.05
ROPE_BASE = 500000.0


def passed_along(value, axis, steps):
    count = lax.axis_size(axis)
    first, last = (max(0, -steps), min(count, count - steps))
    return lax.ppermute(value, axis, [(source, source + steps) for source in range(first, last)])


def split_up(array, dim, length):
    before, after = (array.shape[:dim], array.shape[dim + 1 :])
    return jnp.moveaxis(array.reshape(*before, length, -1, *after), dim, 0)


def summed_on_arrival(array, axis, dim):
    length = lax.axis_size(axis)
    pieces = lax.all_to_all(split_up(array, dim, length), axis, 0, 0, tiled=True)
    return jnp.sum(pieces, axis=0)


def edges_of(length, count):
    unit = 8 if length >= 8 * count else 1
    return [length // unit * k // count * unit for k in range(1, count)]


def joined_along(pieces, dim):
    pieces = jnp.moveaxis(pieces, 0, dim)
    dims = pieces.shape
    return pieces.reshape(*dims[:dim], dims[dim] * dims[dim + 1], *dims[dim + 2 :])


def exchange_in_pieces(array, axis, pieces, split_dim, concat_dim):
    blocks = split_up(array, split_dim, lax.axis_size(axis))
    cut = max(range(1, max(2, blocks.ndim - 1)), key=lambda d: blocks.shape[d])
    outs = []
    for piece in jnp.split(blocks, edges_of(blocks.shape[cut], pieces), axis=cut):
        if piece.size:
            outs.append(lax.all_to_all(piece, axis, split_axis=0, concat_axis=0, tiled=True))
    return joined_along(jnp.concatenate(outs, axis=cut), concat_dim)


def sent_together(arrays, axis, dim, along):
    ends, at = ([], 0)
    for a in arrays[:-1]:
        at += a.shape[along]
        ends.append(at)
    both = jnp.concatenate(arrays, axis=along)
    return tuple(jnp.split(lax.all_gather(both, axis, axis=dim, tiled=True), ends, axis=along))


def rope_tables(length, head_size):
    half_size = head_size // 2
    inverse_freq = ROPE_BASE ** (-jnp.arange(half_size, dtype=jnp.float32) * 2.0 / head_size)
    angles = jnp.arange(length, dtype=jnp.float32)[:, None] * inverse_freq[None, :]
    return (jnp.cos(angles), jnp.sin(angles))


def rotate(values, cosine, sine_table):
    half_size = values.shape[-1] // 2
    first_half = values[..., :half_size]
    second = values[..., half_size:]
    cosine = cosine[None, :, None, :]
    sine_table = sine_table[None, :, None, :]
    return jnp.concatenate(
        [first_half * cosine - second * sine_table, second * cosine + first_half * sine_table],
        axis=-1,
    )


def attend(query_pre, key_pre, value_pre):
    seq_count, length, query_width = query_pre.shape
    query_heads = query_width // HEAD
    kv_heads = key_pre.shape[-1] // HEAD
    group_size = query_heads // kv_heads
    cosine, sine_table = rope_tables(length, HEAD)
    query_vectors = rotate(
        query_pre.reshape(seq_count, length, query_heads, HEAD), cosine, sine_table
    ).astype(jnp.bfloat16)
    key_rows = rotate(
        key_pre.reshape(seq_count, length, kv_heads, HEAD), cosine, sine_table
    ).astype(jnp.bfloat16)
    values = value_pre.reshape(seq_count, length, kv_heads, HEAD).astype(jnp.bfloat16)
    query_vectors = query_vectors.reshape(seq_count, length, kv_heads, group_size, HEAD)
    scores = jnp.einsum(
        "sikge,sjke->skgij", query_vectors.astype(jnp.float32), key_rows.astype(jnp.float32)
    ) * HEAD ** (-0.5)
    causal = (
        jnp.arange(length, dtype=jnp.int32)[:, None] >= jnp.arange(length, dtype=jnp.int32)[None, :]
    )
    scores = jnp.where(causal, scores, -1e30)
    weights = jax.nn.softmax(scores, axis=-1).astype(jnp.bfloat16)
    mixture = jnp.einsum(
        "skgij,sjke->sikge", weights.astype(jnp.float32), values.astype(jnp.float32)
    )
    return mixture.reshape(seq_count, length, query_heads * HEAD)


def normalize(hidden_f, gain_vector):
    inv_rms = lax.rsqrt(jnp.mean(hidden_f * hidden_f, axis=-1, keepdims=True) + EPSILON)
    return hidden_f * inv_rms * gain_vector


def contract_rows(left, right):
    return lax.dot_general(
        left, right, (((0,), (0,)), ((), ())), preferred_element_type=jnp.float32
    )


def contract_last(left, right):
    return lax.dot_general(
        left, right, (((left.ndim - 1,), (1,)), ((), ())), preferred_element_type=jnp.float32
    )


def pool_exits(batch_rows, mask_of_valid, counts):
    total_value = jnp.einsum("ki,kiu->ku", mask_of_valid, batch_rows.astype(jnp.float32))
    return total_value / counts[:, None]


def spread_grad(exit_grad, mask_of_valid, counts):
    return mask_of_valid[:, :, None] * (exit_grad / counts[:, None])[:, None, :]


def matryoshka_losses(pooled, positives):
    pair_total = pooled.shape[0]
    target = (jnp.arange(pair_total, dtype=jnp.int32)[None, :] == positives[:, None]).astype(
        jnp.float32
    )
    losses = []
    for level_index in range(WIDTHS):
        leading_width = pooled.shape[-1] // 2**level_index
        query_vectors = pooled[:, 0, :leading_width]
        passage_rows = pooled[:, 1, :leading_width]
        query_vectors = query_vectors * lax.rsqrt(
            jnp.mean(query_vectors * query_vectors, axis=-1, keepdims=True) + 1e-06
        )
        passage_rows = passage_rows * lax.rsqrt(
            jnp.mean(passage_rows * passage_rows, axis=-1, keepdims=True) + 1e-06
        )
        score_matrix = jnp.dot(query_vectors, passage_rows.T, precision=lax.Precision.HIGHEST) / (
            leading_width * SOFTMAX_TEMPER
        )
        picked = jnp.sum(score_matrix * target, axis=-1)
        losses.append(jnp.mean(jax.nn.logsumexp(score_matrix, axis=-1) - picked))
    return jnp.stack(losses)


def pass_along(batch_rows, direction):
    return passed_along(batch_rows, "section", direction)


def forward_section(hidden, gain_vector, query_weight, key_weight, value_weight, out_weight):
    hidden_f = hidden.astype(jnp.float32)
    normed = normalize(hidden_f, gain_vector).astype(jnp.bfloat16)
    mixture = attend(
        jnp.dot(normed, query_weight, preferred_element_type=jnp.float32),
        jnp.dot(normed, key_weight, preferred_element_type=jnp.float32),
        jnp.dot(normed, value_weight, preferred_element_type=jnp.float32),
    ).astype(jnp.bfloat16)
    partial_value = jnp.dot(mixture, out_weight, preferred_element_type=jnp.float32)
    total_value = lax.psum(partial_value.astype(jnp.bfloat16), "mp").astype(jnp.float32)
    return (hidden_f + total_value).astype(jnp.bfloat16)


def backward_section(
    hidden, upstream, gain_vector, query_weight, key_weight, value_weight, out_weight
):
    hidden_f = hidden.astype(jnp.float32)
    inv_rms = lax.rsqrt(jnp.mean(hidden_f * hidden_f, axis=-1, keepdims=True) + EPSILON)
    normed = normalize(hidden_f, gain_vector).astype(jnp.bfloat16)
    out_grad = upstream.astype(jnp.bfloat16)
    mixture_f, pullback = jax.vjp(
        attend,
        jnp.dot(normed, query_weight, preferred_element_type=jnp.float32),
        jnp.dot(normed, key_weight, preferred_element_type=jnp.float32),
        jnp.dot(normed, value_weight, preferred_element_type=jnp.float32),
    )
    mixture = mixture_f.astype(jnp.bfloat16)
    mixture_grad = contract_last(out_grad, out_weight).astype(jnp.bfloat16)
    pulled = pullback(lax.optimization_barrier(mixture_grad).astype(jnp.float32))
    query_grad, key_grad, value_grad = [piece_grad.astype(jnp.bfloat16) for piece_grad in pulled]
    member_grad = (
        contract_last(query_grad, query_weight)
        + contract_last(key_grad, key_weight)
        + contract_last(value_grad, value_weight)
    )
    normed_grad = lax.psum(member_grad.astype(jnp.bfloat16), "mp").astype(jnp.float32)
    rounded = lax.optimization_barrier(member_grad.astype(jnp.bfloat16)).astype(jnp.float32)
    gain_term = jnp.sum(rounded * hidden_f * inv_rms, axis=(0, 1))
    _, norm_pull = jax.vjp(lambda values: normalize(values, gain_vector), hidden_f)
    input_grad = (upstream + norm_pull(normed_grad)[0]).astype(jnp.bfloat16)
    width_all = hidden.shape[-1]
    head_grads = jnp.concatenate([query_grad, key_grad, value_grad], axis=-1)
    stored_now = (
        normed.reshape(-1, width_all),
        out_grad.reshape(-1, width_all),
        head_grads.reshape(-1, head_grads.shape[-1]),
        mixture.reshape(-1, mixture.shape[-1]),
        gain_term,
    )
    return (input_grad, stored_now)


def local(entrance, lengths, positives, norm_gains, query_proj, key_proj, value_proj, out_proj):
    section_count = lax.axis_size("section")
    section_index = lax.axis_index("section")
    pair_count = entrance.shape[0]
    seq_count = 2 * pair_count
    length = entrance.shape[2]
    width_all = entrance.shape[3]
    start_hidden = entrance.reshape(seq_count, length, width_all)
    mask_of_valid = (
        jnp.arange(length, dtype=jnp.int32)[None, :] < lengths.reshape(seq_count, 1)
    ).astype(jnp.float32)
    counts = jnp.sum(mask_of_valid, axis=1)
    gain_vector = norm_gains[0]
    query_weight = query_proj[0]
    key_weight = key_proj[0]
    value_weight = value_proj[0]
    out_weight = out_proj[0]
    current = start_hidden
    saved_input = start_hidden
    exit_rows = start_hidden
    for section_turn in range(section_count):
        produced = forward_section(
            current, gain_vector, query_weight, key_weight, value_weight, out_weight
        )
        chosen = section_index == section_turn
        saved_input = jnp.where(chosen, current, saved_input)
        exit_rows = jnp.where(chosen, produced, exit_rows)
        if section_turn + 1 < section_count:
            arrived = pass_along(produced, 1)
            current = jnp.where(section_index == 0, start_hidden, arrived)
    pooled = pool_exits(exit_rows, mask_of_valid, counts).reshape(pair_count, 2, width_all)
    gathered = lax.all_gather(pooled.astype(jnp.bfloat16), "dp", axis=0, tiled=True).astype(
        pooled.dtype
    )
    losses_now, pullback = jax.vjp(
        lambda embedded: matryoshka_losses(embedded, positives), gathered
    )
    pair_grads = pullback(jnp.ones((WIDTHS,), jnp.float32))[0]
    own_losses = losses_now[None]
    own_grad = lax.dynamic_slice_in_dim(
        pair_grads, lax.axis_index("dp") * pair_count, pair_count, 0
    )
    token_grad = spread_grad(own_grad.reshape(seq_count, width_all), mask_of_valid, counts)
    incoming = jnp.zeros(start_hidden.shape, jnp.bfloat16)
    stored = None
    for section_turn in range(section_count):
        owner_section = section_count - 1 - section_turn
        upstream = token_grad + incoming.astype(jnp.float32)
        input_grad, stored_now = backward_section(
            saved_input, upstream, gain_vector, query_weight, key_weight, value_weight, out_weight
        )
        chosen = section_index == owner_section
        if stored is None:
            stored = stored_now
        else:
            stored = jax.tree.map(
                lambda fresh, former: jnp.where(chosen, fresh, former), stored_now, stored
            )
        if section_turn + 1 < section_count:
            incoming = pass_along(input_grad, -1)
    normed_rows, out_rows, head_grads, mixture_rows, gain_term = stored
    gain_share = summed_on_arrival(gain_term, ("dp", "mp"), 0)
    normed_cols, out_cols = (
        exchange_in_pieces(normed_rows, "dp", 2, 1, 0),
        exchange_in_pieces(out_rows, "dp", 2, 1, 0),
    )
    head_piece, mixture_piece = sent_together((head_grads, mixture_rows), "dp", 0, 1)
    weight_sums = jnp.concatenate(
        [contract_rows(normed_cols, head_piece), contract_rows(out_cols, mixture_piece)], axis=1
    )
    query_cols = query_weight.shape[1]
    kv_cols = key_weight.shape[1]
    query_grad_out = weight_sums[:, :query_cols][None]
    key_grad_out = weight_sums[:, query_cols : query_cols + kv_cols][None]
    value_grad_out = weight_sums[:, query_cols + kv_cols : query_cols + 2 * kv_cols][None]
    out_grad_out = weight_sums[:, query_cols + 2 * kv_cols :].T[None]
    return (
        own_losses,
        gain_share[None],
        query_grad_out,
        key_grad_out,
        value_grad_out,
        out_grad_out,
    )


def solution(mesh):
    in_specs = (
        P("dp", None, None, None),
        P("dp", None),
        P(),
        P("section", None),
        P("section", None, "mp"),
        P("section", None, "mp"),
        P("section", None, "mp"),
        P("section", "mp", None),
    )
    out_specs = (
        P("section", None),
        P("section", ("dp", "mp")),
        P("section", "dp", "mp"),
        P("section", "dp", "mp"),
        P("section", "dp", "mp"),
        P("section", "mp", "dp"),
    )
    return jax.shard_map(local, mesh=mesh, in_specs=in_specs, out_specs=out_specs, check_vma=False)
```

profile of v0, /device:TPU:32, one launch (start us, length us, event | category | flops | bytes accessed | tf_op | source)
XLA Modules:
  0.0 795.2 jit_solution(6946934551017990552)
XLA Ops:
  7.3 1.9 fusion.24
  9.2 6.6 copy.215
  16.0 3.8 fusion.80
  22.3 4.3 convolution_convert_fusion.3
  26.7 52.6 %all-reduce.38.cloned.1.call-done = bf16[2,96,4096]{2,1,0:T(8,128)(2,1)} async-done(((bf16[2,96,4096]{2,1,0:T(8,128)(2,1)}), bf16[2,96,4096]{2,1,0:T(8,128)(2,1)}) %all-reduce.38.cloned.1.call-update) | async-done | bytes 1572880 | tf_op jit(solution)/shard_map/psum | solution.py:170
  79.3 3.1 fusion.25
  82.4 1.9 collective-permute-start
  84.3 20.1 %collective-permute-done = bf16[2,96,4096]{2,1,0:T(8,128)(2,1)} collective-permute-done((bf16[2,96,4096]{2,1,0:T(8,128)(2,1)}, bf16[2,96,4096]{2,1,0:T(8,128)(2,1)}, u32[]{:S(2)}, u32[]{:S(2)}) %collective-permute-start) | collective-permute-done | bytes 1572896 | tf_op jit(solution)/shard_map/ppermute | solution.py:16
  104.5 2.1 fusion.26
  109.8 2.2 fusion.131
  112.3 4.3 convolution_convert_fusion.2
  116.7 50.4 %all-reduce.40.cloned.1.call-done = bf16[2,96,4096]{2,1,0:T(8,128)(2,1)} async-done(((bf16[2,96,4096]{2,1,0:T(8,128)(2,1)}), bf16[2,96,4096]{2,1,0:T(8,128)(2,1)}) %all-reduce.40.cloned.1.call-update) | async-done | bytes 1572880 | tf_op jit(solution)/shard_map/psum | solution.py:170
  167.1 2.4 fusion.29
  169.5 2.5 collective-permute-start.1
  172.0 19.5 %collective-permute-done.1 = bf16[2,96,4096]{2,1,0:T(8,128)(2,1)S(1)} collective-permute-done((bf16[2,96,4096]{2,1,0:T(8,128)(2,1)S(1)}, bf16[2,96,4096]{2,1,0:T(8,128)(2,1)S(1)}, u32[]{:S(2)}, u32[]{:S(2)}) %collective-permute-start.1) | collective-permute-done | bytes 1572896 | tf_op jit(solution)/shard_map/ppermute | solution.py:16
  195.5 2.2 fusion.132
  197.9 4.5 convolution_convert_fusion.1
  202.5 50.4 %all-reduce.42.cloned.1.call-done = bf16[2,96,4096]{2,1,0:T(8,128)(2,1)} async-done(((bf16[2,96,4096]{2,1,0:T(8,128)(2,1)}), bf16[2,96,4096]{2,1,0:T(8,128)(2,1)}) %all-reduce.42.cloned.1.call-update) | async-done | bytes 1572880 | tf_op jit(solution)/shard_map/psum | solution.py:170
  252.9 3.1 fusion.33
  256.0 1.9 collective-permute-start.2
  258.0 20.1 %collective-permute-done.2 = bf16[2,96,4096]{2,1,0:T(8,128)(2,1)} collective-permute-done((bf16[2,96,4096]{2,1,0:T(8,128)(2,1)}, bf16[2,96,4096]{2,1,0:T(8,128)(2,1)}, u32[]{:S(2)}, u32[]{:S(2)}) %collective-permute-start.2) | collective-permute-done | bytes 1572896 | tf_op jit(solution)/shard_map/ppermute | solution.py:16
  278.1 3.7 fusion.44
  282.6 2.5 copy-done.43
  291.8 2.2 fusion.133
  294.3 4.5 convolution_convert_fusion
  300.4 2.0 fusion.152
  302.4 46.9 %all-reduce.44.cloned.1.call-done = bf16[2,96,4096]{2,1,0:T(8,128)(2,1)} async-done(((bf16[2,96,4096]{2,1,0:T(8,128)(2,1)}), bf16[2,96,4096]{2,1,0:T(8,128)(2,1)}) %all-reduce.44.cloned.1.call-update) | async-done | bytes 1572880 | tf_op jit(solution)/shard_map/psum | solution.py:170
  349.3 4.7 fusion.68
  354.1 34.6 %all-gather.1 = bf16[8,2,4096]{2,1,0:T(2,128)(2,1)S(1)} all-gather(bf16[1,2,4096]{2,1,0:T(2,128)(2,1)S(1)} %fusion.387), channel_id=2, replica_groups=mesh['section'=4,'dp'=8,'mp'=4] {'dp'}, dimensions={0}, use_global_device_ids=true | all-gather | bytes 147456 | tf_op jit(solution)/shard_map/all_gather | solution.py:244
  402.0 2.2 fusion.105
  414.3 50.1 %all-reduce.46.cloned.1.call-done = bf16[2,96,4096]{2,1,0:T(8,128)(2,1)} async-done(((bf16[2,96,4096]{2,1,0:T(8,128)(2,1)}), bf16[2,96,4096]{2,1,0:T(8,128)(2,1)}) %all-reduce.46.cloned.1.call-update) | async-done | bytes 1572880 | tf_op jit(solution)/shard_map/psum | solution.py:196
  464.4 2.1 fusion.47
  468.4 2.2 collective-permute-start.3
  470.6 17.7 %collective-permute-done.3 = bf16[2,96,4096]{2,1,0:T(8,128)(2,1)S(1)} collective-permute-done((bf16[2,96,4096]{2,1,0:T(8,128)(2,1)S(1)}, bf16[2,96,4096]{2,1,0:T(8,128)(2,1)S(1)}, u32[]{:S(2)}, u32[]{:S(2)}) %collective-permute-start.3) | collective-permute-done | bytes 1572896 | tf_op jit(solution)/shard_map/ppermute | solution.py:16
  491.2 2.2 fusion.108
  504.3 51.8 %all-reduce.48.cloned.1.call-done = bf16[2,96,4096]{2,1,0:T(8,128)(2,1)} async-done(((bf16[2,96,4096]{2,1,0:T(8,128)(2,1)}), bf16[2,96,4096]{2,1,0:T(8,128)(2,1)}) %all-reduce.48.cloned.1.call-update) | async-done | bytes 1572880 | tf_op jit(solution)/shard_map/psum | solution.py:196
  556.1 2.2 fusion.48
  559.9 1.9 collective-permute-start.4
  561.8 17.9 %collective-permute-done.4 = bf16[2,96,4096]{2,1,0:T(8,128)(2,1)S(1)} collective-permute-done((bf16[2,96,4096]{2,1,0:T(8,128)(2,1)S(1)}, bf16[2,96,4096]{2,1,0:T(8,128)(2,1)S(1)}, u32[]{:S(2)}, u32[]{:S(2)}) %collective-permute-start.4) | collective-permute-done | bytes 1572896 | tf_op jit(solution)/shard_map/ppermute | solution.py:16
  582.7 2.3 fusion.111
  594.1 1.8 fusion.2
  596.1 51.6 %all-reduce.50.cloned.1.call-done = bf16[2,96,4096]{2,1,0:T(8,128)(2,1)} async-done(((bf16[2,96,4096]{2,1,0:T(8,128)(2,1)}), bf16[2,96,4096]{2,1,0:T(8,128)(2,1)}) %all-reduce.50.cloned.1.call-update) | async-done | bytes 1572880 | tf_op jit(solution)/shard_map/psum | solution.py:196
  647.7 2.2 fusion.49
  651.6 2.1 collective-permute-start.5
  657.7 13.8 %collective-permute-done.5 = bf16[2,96,4096]{2,1,0:T(8,128)(2,1)S(1)} collective-permute-done((bf16[2,96,4096]{2,1,0:T(8,128)(2,1)S(1)}, bf16[2,96,4096]{2,1,0:T(8,128)(2,1)S(1)}, u32[]{:S(2)}, u32[]{:S(2)}) %collective-permute-start.5) | collective-permute-done | bytes 1572896 | tf_op jit(solution)/shard_map/ppermute | solution.py:16
  673.3 2.2 fusion.114
  681.5 2.1 copy.221
  685.3 6.5 all-to-all-start.2
  692.1 4.4 copy.230
  696.5 1.8 copy.229
  698.3 1.9 copy.228
  704.9 1.9 fusion.57
  706.9 7.5 all-to-all-start.1
  715.0 2.4 copy.227
  717.4 6.9 fusion.66
  725.4 7.7 all-to-all-start
  733.1 2.4 fusion.658
  735.5 7.5 all-to-all-done
  742.9 16.8 %all_to_all.26 = bf16[8,96,512]{2,1,0:T(8,128)(2,1)} all-to-all(bf16[8,96,512]{2,1,0:T(8,128)(2,1)S(1)} %get-tuple-element.62), channel_id=1, replica_groups=mesh['section'=4,'dp'=8,'mp'=4] {'dp'}, dimensions={0} | all-to-all | bytes 1572864 | tf_op jit(solution)/shard_map/all_to_all | solution.py:47
  759.8 6.2 all-to-all-start.3
  772.8 4.3 all-to-all-done.3
  777.0 2.6 pad_maximum_fusion.1
  779.7 3.2 fusion.61
  784.8 3.4 fusion.97
  (481 shorter events, 97.2 us)
Async XLA Ops:
  7.2 14.1 %copy-start = (bf16[1,4096,128]{2,1,0:T(8,128)(2,1)S(1)}, bf16[1,4096,128]{2,1,0:T(8,128)(2,1)}, u32[]{:S(2)}) copy-start(bf16[1,4096,128]{2,1,0:T(8,128)(2,1)} %param.14) | copy-start | bytes 3145732
  7.2 72.1 %all-reduce.38.cloned.1.call-start = ((), (), s32[]{:S(2)}) async-start(), calls=%async_computation.5 | async-start | bytes 3145728 | tf_op jit(solution)/shard_map/psum | solution.py:170
  7.3 292.7 %copy-start.70 = (pred[96,96]{0,1:T(8,128)(4,1)}, pred[96,96]{0,1:T(8,128)(4,1)S(1)}, u32[]{:S(2)}) copy-start(pred[96,96]{0,1:T(8,128)(4,1)S(1)} %iota_compare_fusion) | copy-start | bytes 27652
  9.2 6.8 copy-start.9
  9.2 6.8 copy-start.58
  26.7 140.4 %all-reduce.40.cloned.1.call-start = ((), (), s32[]{:S(2)}) async-start(), calls=%async_computation.6 | async-start | bytes 3145728 | tf_op jit(solution)/shard_map/psum | solution.py:170
  82.4 22.0 %collective-permute-start = (bf16[2,96,4096]{2,1,0:T(8,128)(2,1)}, bf16[2,96,4096]{2,1,0:T(8,128)(2,1)}, u32[]{:S(2)}, u32[]{:S(2)}) collective-permute-start(bf16[2,96,4096]{2,1,0:T(8,128)(2,1)} %fusion.25), channel_id=1, source_target_pairs={{0,32},{32,64},{64,96},{1,33},{33,65},{65,97},{2,34},{34,66},{66,9... | collective-permute-start | bytes 4718600 | tf_op jit(solution)/shard_map/ppermute | solution.py:16
  84.3 22.3 %copy-start.41 = (bf16[512,4096]{1,0:T(8,128)(2,1)S(1)}, bf16[512,4096]{1,0:T(8,128)(2,1)}, u32[]{:S(2)}) copy-start(bf16[512,4096]{1,0:T(8,128)(2,1)} %copy.215) | copy-start | bytes 12582916
  116.6 136.3 %all-reduce.42.cloned.1.call-start = ((), (), s32[]{:S(2)}) async-start(), calls=%async_computation.7 | async-start | bytes 3145728 | tf_op jit(solution)/shard_map/psum | solution.py:170
  169.5 22.8 %copy-start.54 = (bf16[2,96,4096]{2,1,0:T(8,128)(2,1)}, bf16[2,96,4096]{2,1,0:T(8,128)(2,1)S(1)}, u32[]{:S(2)}) copy-start(bf16[2,96,4096]{2,1,0:T(8,128)(2,1)S(1)} %fusion.29) | copy-start | bytes 4718596
  169.5 22.8 %copy-start.42 = (bf16[512,4096]{1,0:T(8,128)(2,1)S(1)}, bf16[512,4096]{1,0:T(8,128)(2,1)}, u32[]{:S(2)}) copy-start(bf16[512,4096]{1,0:T(8,128)(2,1)} %copy.215) | copy-start | bytes 12582916
  169.5 22.0 %collective-permute-start.1 = (bf16[2,96,4096]{2,1,0:T(8,128)(2,1)S(1)}, bf16[2,96,4096]{2,1,0:T(8,128)(2,1)S(1)}, u32[]{:S(2)}, u32[]{:S(2)}) collective-permute-start(bf16[2,96,4096]{2,1,0:T(8,128)(2,1)S(1)} %fusion.29), channel_id=1, source_target_pairs={{0,32},{32,64},{64,96},{1,33},{33,65},{65,97},{2,34},{34,66},{66,9... | collective-permute-start | bytes 4718600 | tf_op jit(solution)/shard_map/ppermute | solution.py:16
  197.9 55.0 %copy-start.24 = (bf16[2,96,4096]{2,1,0:T(8,128)(2,1)S(1)}, bf16[2,96,4096]{2,1,0:T(8,128)(2,1)}, u32[]{:S(2)}) copy-start(bf16[2,96,4096]{2,1,0:T(8,128)(2,1)} %copy-done.23) | copy-start | bytes 4718596
  202.4 146.9 %all-reduce.44.cloned.1.call-start = ((), (), s32[]{:S(2)}) async-start(), calls=%async_computation.8 | async-start | bytes 3145728 | tf_op jit(solution)/shard_map/psum | solution.py:170
  256.0 22.0 %collective-permute-start.2 = (bf16[2,96,4096]{2,1,0:T(8,128)(2,1)}, bf16[2,96,4096]{2,1,0:T(8,128)(2,1)}, u32[]{:S(2)}, u32[]{:S(2)}) collective-permute-start(bf16[2,96,4096]{2,1,0:T(8,128)(2,1)} %fusion.33), channel_id=1, source_target_pairs={{0,32},{32,64},{64,96},{1,33},{33,65},{65,97},{2,34},{34,66},{66,9... | collective-permute-start | bytes 4718600 | tf_op jit(solution)/shard_map/ppermute | solution.py:16
  281.8 4.9 copy-start.118
  281.8 7.1 copy-start.40
  281.8 4.8 copy-start.107
  282.6 4.0 copy-start.18
  294.2 4.6 copy-start.122
  294.2 5.4 copy-start.96
  294.2 5.4 copy-start.97
  294.2 5.5 copy-start.62
  294.3 5.5 copy-start.63
  298.8 165.7 %all-reduce.46.cloned.1.call-start = ((), (), s32[]{:S(2)}) async-start(), calls=%async_computation.9 | async-start | bytes 3145728 | tf_op jit(solution)/shard_map/psum | solution.py:196
  299.0 55.0 %copy-start.120 = (f32[2]{0:T(128)}, f32[2]{0:T(128)S(1)}, u32[]{:S(2)}) copy-start(f32[2]{0:T(128)S(1)} %fusion.646) | copy-start | bytes 28
  299.9 107.5 %copy-start.64 = (bf16[2,96,4,128]{3,1,2,0:T(8,128)(2,1)}, bf16[2,96,4,128]{3,1,2,0:T(8,128)(2,1)S(1)}, u32[]{:S(2)}) copy-start(bf16[2,96,4,128]{3,1,2,0:T(8,128)(2,1)S(1)} %pad_maximum_fusion.3) | copy-start | bytes 589828
  300.2 107.2 %copy-start.98 = (f32[2,4,96]{2,1,0:T(4,128)}, f32[2,4,96]{2,1,0:T(4,128)S(1)}, u32[]{:S(2)}) copy-start(f32[2,4,96]{2,1,0:T(4,128)S(1)} %get-tuple-element.182) | copy-start | bytes 9220
  300.4 53.6 %copy-start.113 = (f32[2,4,96]{2,1,0:T(4,128)}, f32[2,4,96]{2,1,0:T(4,128)S(1)}, u32[]{:S(2)}) copy-start(f32[2,4,96]{2,1,0:T(4,128)S(1)} %fusion.647) | copy-start | bytes 9220
  300.4 105.5 %copy-start.100 = (f32[2,4,96]{2,1,0:T(4,128)}, f32[2,4,96]{2,1,0:T(4,128)S(1)}, u32[]{:S(2)}) copy-start(f32[2,4,96]{2,1,0:T(4,128)S(1)} %multiply_divide_fusion) | copy-start | bytes 9220
  302.4 103.5 %copy-start.55 = (bf16[2,96,128,1]{2,1,3,0:T(8,128)(2,1)}, bf16[2,96,128,1]{2,1,3,0:T(8,128)(2,1)S(1)}, u32[]{:S(2)}) copy-start(bf16[2,96,128,1]{2,1,3,0:T(8,128)(2,1)S(1)} %fusion.152) | copy-start | bytes 147460
  349.3 42.8 %copy-start.112 = (s32[8]{0:T(128)S(1)}, s32[8]{0:T(128)}, u32[]{:S(2)}) copy-start(s32[8]{0:T(128)} %param.10) | copy-start | bytes 100
  388.7 13.1 %copy-start.121 = (f32[2]{0:T(128)S(1)}, f32[2]{0:T(128)}, u32[]{:S(2)}) copy-start(f32[2]{0:T(128)} %copy-done.120) | copy-start | bytes 28
  388.7 13.2 %copy-start.5 = (bf16[1,512,4096]{2,1,0:T(8,128)(2,1)S(1)}, bf16[1,512,4096]{2,1,0:T(8,128)(2,1)}, u32[]{:S(2)}) copy-start(bf16[1,512,4096]{2,1,0:T(8,128)(2,1)} %param.15) | copy-start | bytes 12582916
  388.7 13.2 %copy-start.102 = (f32[2,96]{1,0:T(2,128)S(1)}, f32[2,96]{1,0:T(2,128)}, u32[]{:S(2)}) copy-start(f32[2,96]{1,0:T(2,128)} %get-tuple-element.123) | copy-start | bytes 2308
  401.9 5.2 copy-start.71
  402.0 5.2 copy-start.94
  408.4 4.1 copy-start.79
  414.3 141.8 %all-reduce.48.cloned.1.call-start = ((), (), s32[]{:S(2)}) async-start(), calls=%async_computation.10 | async-start | bytes 3145728 | tf_op jit(solution)/shard_map/psum | solution.py:196
  467.2 24.1 %copy-start.6 = (bf16[1,512,4096]{2,1,0:T(8,128)(2,1)S(1)}, bf16[1,512,4096]{2,1,0:T(8,128)(2,1)}, u32[]{:S(2)}) copy-start(bf16[1,512,4096]{2,1,0:T(8,128)(2,1)} %param.15) | copy-start | bytes 12582916
  468.4 20.0 %collective-permute-start.3 = (bf16[2,96,4096]{2,1,0:T(8,128)(2,1)S(1)}, bf16[2,96,4096]{2,1,0:T(8,128)(2,1)S(1)}, u32[]{:S(2)}, u32[]{:S(2)}) collective-permute-start(bf16[2,96,4096]{2,1,0:T(8,128)(2,1)S(1)} %fusion.42), channel_id=1, source_target_pairs={{32,0},{64,32},{96,64},{33,1},{65,33},{97,65},{34,2},{66,34},{98,6... | collective-permute-start | bytes 4718600 | tf_op jit(solution)/shard_map/ppermute | solution.py:16
  504.3 143.4 %all-reduce.50.cloned.1.call-start = ((), (), s32[]{:S(2)}) async-start(), calls=%async_computation.11 | async-start | bytes 3145728 | tf_op jit(solution)/shard_map/psum | solution.py:196
  558.5 24.2 %copy-start.7 = (bf16[1,512,4096]{2,1,0:T(8,128)(2,1)S(1)}, bf16[1,512,4096]{2,1,0:T(8,128)(2,1)}, u32[]{:S(2)}) copy-start(bf16[1,512,4096]{2,1,0:T(8,128)(2,1)} %param.15) | copy-start | bytes 12582916
  559.9 19.8 %collective-permute-start.4 = (bf16[2,96,4096]{2,1,0:T(8,128)(2,1)S(1)}, bf16[2,96,4096]{2,1,0:T(8,128)(2,1)S(1)}, u32[]{:S(2)}, u32[]{:S(2)}) collective-permute-start(bf16[2,96,4096]{2,1,0:T(8,128)(2,1)S(1)} %fusion.39), channel_id=1, source_target_pairs={{32,0},{64,32},{96,64},{33,1},{65,33},{97,65},{34,2},{66,34},{98,6... | collective-permute-start | bytes 4718600 | tf_op jit(solution)/shard_map/ppermute | solution.py:16
  595.9 183.8 %all-gather.4.cloned.1.call-start = ((), (), s32[]{:S(2)}) async-start(), calls=%async_computation.12 | async-start | bytes 4423680 | tf_op jit(solution)/shard_map/all_gather | solution.py:57
  650.1 4.7 copy-start.45
  650.1 5.6 copy-start.47
  650.1 5.6 copy-start.49
  651.5 5.2 copy-start.51
  651.6 5.2 copy-start.53
  651.6 20.0 %collective-permute-start.5 = (bf16[2,96,4096]{2,1,0:T(8,128)(2,1)S(1)}, bf16[2,96,4096]{2,1,0:T(8,128)(2,1)S(1)}, u32[]{:S(2)}, u32[]{:S(2)}) collective-permute-start(bf16[2,96,4096]{2,1,0:T(8,128)(2,1)S(1)} %fusion.41), channel_id=1, source_target_pairs={{32,0},{64,32},{96,64},{33,1},{65,33},{97,65},{34,2},{66,34},{98,6... | collective-permute-start | bytes 4718600 | tf_op jit(solution)/shard_map/ppermute | solution.py:16
  655.7 17.5 %copy-start.8 = (bf16[1,512,4096]{2,1,0:T(8,128)(2,1)S(1)}, bf16[1,512,4096]{2,1,0:T(8,128)(2,1)}, u32[]{:S(2)}) copy-start(bf16[1,512,4096]{2,1,0:T(8,128)(2,1)} %param.15) | copy-start | bytes 12582916
  673.2 4.0 copy-start.99
  673.2 4.0 copy-start.101
  673.2 5.3 copy-start.72
  673.2 5.3 copy-start.95
  673.3 5.3 copy-start.115
  685.3 21.6 %all-to-all-start.2 = ((bf16[8,96,512]{2,1,0:T(8,128)(2,1)}), bf16[8,96,512]{2,1,0:T(8,128)(2,1)}, u32[]{:S(2)}, u32[]{:S(2)}) async-start(bf16[8,96,512]{2,1,0:T(8,128)(2,1)} %get-tuple-element.66), calls=%async_computation.2 | async-start | bytes 1572864 | tf_op jit(solution)/shard_map/all_to_all | solution.py:47
  692.1 4.4 copy-start.27
  706.9 10.6 %copy-start.39 = (bf16[24,8,8,512]{3,2,1,0:T(8,128)(2,1)S(1)}, bf16[24,8,8,512]{3,2,1,0:T(8,128)(2,1)}, u32[]{:S(2)}) copy-start(bf16[24,8,8,512]{3,2,1,0:T(8,128)(2,1)} %copy.229) | copy-start | bytes 4718596
  706.9 18.5 %all-to-all-start.1 = ((bf16[8,96,512]{2,1,0:T(8,128)(2,1)}), bf16[8,96,512]{2,1,0:T(8,128)(2,1)S(1)}, u32[]{:S(2)}, u32[]{:S(2)}) async-start(bf16[8,96,512]{2,1,0:T(8,128)(2,1)} %get-tuple-element.65), calls=%async_computation.1 | async-start | bytes 1572864 | tf_op jit(solution)/shard_map/all_to_all | solution.py:47
  725.4 17.6 %all-to-all-start = ((f32[32,1,128]{2,1,0:T(1,128)}), f32[32,1,128]{2,1,0:T(1,128)S(1)}, u32[]{:S(2)}, u32[]{:S(2)}) async-start(f32[32,1,128]{2,1,0:T(1,128)} %bitcast.213), calls=%async_computation | async-start | bytes 32768 | tf_op jit(solution)/shard_map/all_to_all | solution.py:26
  759.8 17.2 %all-to-all-start.3 = ((bf16[8,96,512]{2,1,0:T(8,128)(2,1)}), bf16[8,96,512]{2,1,0:T(8,128)(2,1)}, u32[]{:S(2)}, u32[]{:S(2)}) async-start(bf16[8,96,512]{2,1,0:T(8,128)(2,1)} %get-tuple-element.61), calls=%async_computation.3 | async-start | bytes 1572864 | tf_op jit(solution)/shard_map/all_to_all | solution.py:47
  779.7 5.2 copy-start.38
  (77 other events, 164.9 us)
Sparse Core Ops, SparseCore 0:
  26.8 52.4 all-reduce.37
  116.8 50.2 all-reduce.39
  202.6 50.3 all-reduce.41
  298.9 50.3 all-reduce.43
  414.4 49.9 all-reduce.45
  504.4 51.6 all-reduce.47
  596.0 51.6 all-reduce.49
  681.5 85.7 all-gather.3
where the time goes:
time: 805 us; the launch traced here: 795 us
  waiting for transfers between devices  476 us (59%)
  matrix products  95.4 us (12%)
  other arithmetic  58.7 us (7%)
  local copies, waits for them, and re-layouts  51.7 us (6%)
  blocking collectives  51.5 us (6%)
  starting transfers between devices  40.9 us (5%)
  between operations  21.1 us (3%)
    psum x4, waiting for transfers between devices, forward_section(): lax.psum(partial_value.astype(jnp.bfloat16), 'mp').astype(jnp.float32)  200 us
    psum x3, waiting for transfers between devices, backward_section(): lax.psum(member_grad.astype(jnp.bfloat16), 'mp').astype(jnp.float32)  154 us
    ppermute x6, waiting for transfers between devices, passed_along(): lax.ppermute(value, axis, [(source, source + steps) for source in range(f...  109 us
    all_gather x1, blocking collectives, local(): lax.all_gather(pooled.astype(jnp.bfloat16), 'dp', axis=0, tiled=True)  34.6 us
    unnamed x256, local copies, waits for them, and re-layouts  30.1 us
    dot_general x16, matrix products, contract_last(): lax.dot_general(left, right, (((left.ndim - 1,), (1,)), ((), ())), prefer...  23.3 us
    all_to_all x3, starting transfers between devices, exchange_in_pieces(): lax.all_to_all(piece, axis, split_axis=0, concat_axis=0, tiled=True)  20.2 us
    dot_general x4, matrix products, forward_section(): jnp.dot(mixture, out_weight, preferred_element_type=jnp.float32)  17.6 us
  transfers between devices with their start and end apart: 18, of which 16 were waited for; matrix products, arithmetic and copies ran while one was open for 5% of the time, Pallas kernels for 0%

commit v1 on v0

--- a/solution.py
+++ b/solution.py
@@ -159,6 +159,10 @@
 
 
 def forward_section(hidden, gain_vector, query_weight, key_weight, value_weight, out_weight):
+
+    def _list_floor(page, peer_axis):
+        return lax.all_gather(page, peer_axis).sum(axis=0)
+
     hidden_f = hidden.astype(jnp.float32)
     normed = normalize(hidden_f, gain_vector).astype(jnp.bfloat16)
     mixture = attend(
@@ -167,7 +171,7 @@
         jnp.dot(normed, value_weight, preferred_element_type=jnp.float32),
     ).astype(jnp.bfloat16)
     partial_value = jnp.dot(mixture, out_weight, preferred_element_type=jnp.float32)
-    total_value = lax.psum(partial_value.astype(jnp.bfloat16), "mp").astype(jnp.float32)
+    total_value = _list_floor(partial_value.astype(jnp.bfloat16), "mp").astype(jnp.float32)
     return (hidden_f + total_value).astype(jnp.bfloat16)
 
 

time: 805 us -> 890 us (1.11)
  waiting for transfers between devices: 476 us -> 538 us
  other arithmetic: 58.7 us -> 81.2 us
    all_gather x0 -> x4, waiting for transfers between devices: none -> 263 us  [_list_floor(): return lax.all_gather(page, peer_axis).sum(axis=0)]
    psum x4 -> x0, waiting for transfers between devices: 200 us -> none  [forward_section(): lax.psum(partial_value.astype(jnp.bfloat16), 'mp').astype(jnp.float32)]
    reduce_sum x0 -> x4, other arithmetic: none -> 22.5 us  [_list_floor(): return lax.all_gather(page, peer_axis).sum(axis=0)]
where the time goes in v1:
time: 890 us; the launch traced here: 882 us
  waiting for transfers between devices  538 us (60%)
  matrix products  95.2 us (11%)
  other arithmetic  81.2 us (9%)
  blocking collectives  54.2 us (6%)
  local copies, waits for them, and re-layouts  51.7 us (6%)
  starting transfers between devices  41.1 us (5%)
  between operations  21.2 us (2%)
    all_gather x4, waiting for transfers between devices, _list_floor(): return lax.all_gather(page, peer_axis).sum(axis=0)  263 us
    psum x3, waiting for transfers between devices, backward_section(): lax.psum(member_grad.astype(jnp.bfloat16), 'mp').astype(jnp.float32)  154 us
    ppermute x6, waiting for transfers between devices, passed_along(): lax.ppermute(value, axis, [(source, source + steps) for source in range(f...  108 us
    all_gather x1, blocking collectives, local(): lax.all_gather(pooled.astype(jnp.bfloat16), 'dp', axis=0, tiled=True)  34.3 us
    unnamed x256, local copies, waits for them, and re-layouts  30.1 us
    dot_general x16, matrix products, contract_last(): lax.dot_general(left, right, (((left.ndim - 1,), (1,)), ((), ())), prefer...  23.3 us
    reduce_sum x4, other arithmetic, _list_floor(): return lax.all_gather(page, peer_axis).sum(axis=0)  22.5 us
    all_to_all x1, blocking collectives, exchange_in_pieces(): lax.all_to_all(piece, axis, split_axis=0, concat_axis=0, tiled=True)  19.9 us
  transfers between devices with their start and end apart: 18, of which 16 were waited for; matrix products, arithmetic and copies ran while one was open for 5% of the time, Pallas kernels for 0%

profile of v1, /device:TPU:32, one launch (start us, length us, event | category | flops | bytes accessed | tf_op | source)
XLA Modules:
  0.0 882.2 jit_solution(14673104632840676197)
XLA Ops:
  9.2 6.5 copy.215
  15.9 3.8 fusion.80
  22.3 4.3 convolution_convert_fusion.3
  26.7 67.8 %all-gather.14.cloned.1.call-done = bf16[8,96,4096]{2,1,0:T(8,128)(2,1)} async-done(((bf16[2,96,4096]{2,1,0:T(8,128)(2,1)}), bf16[8,96,4096]{2,1,0:T(8,128)(2,1)}) %all-gather.14.cloned.1.call-update) | async-done | bytes 6291472 | tf_op jit(solution)/shard_map/all_gather | solution.py:164
  94.5 5.6 reduce_sum.688
  100.1 3.1 fusion.25
  103.2 2.4 collective-permute-start
  105.7 19.6 %collective-permute-done = bf16[2,96,4096]{2,1,0:T(8,128)(2,1)} collective-permute-done((bf16[2,96,4096]{2,1,0:T(8,128)(2,1)}, bf16[2,96,4096]{2,1,0:T(8,128)(2,1)}, u32[]{:S(2)}, u32[]{:S(2)}) %collective-permute-start) | collective-permute-done | bytes 1572896 | tf_op jit(solution)/shard_map/ppermute | solution.py:16
  125.2 2.1 fusion.26
  130.6 2.2 fusion.131
  133.1 4.3 convolution_convert_fusion.2
  137.4 66.2 %all-gather.16.cloned.1.call-done = bf16[8,96,4096]{2,1,0:T(8,128)(2,1)} async-done(((bf16[2,96,4096]{2,1,0:T(8,128)(2,1)}), bf16[8,96,4096]{2,1,0:T(8,128)(2,1)}) %all-gather.16.cloned.1.call-update) | async-done | bytes 6291472 | tf_op jit(solution)/shard_map/all_gather | solution.py:164
  203.7 5.6 reduce_sum.694
  209.3 2.4 fusion.29
  211.7 2.5 collective-permute-start.1
  214.2 19.5 %collective-permute-done.1 = bf16[2,96,4096]{2,1,0:T(8,128)(2,1)S(1)} collective-permute-done((bf16[2,96,4096]{2,1,0:T(8,128)(2,1)S(1)}, bf16[2,96,4096]{2,1,0:T(8,128)(2,1)S(1)}, u32[]{:S(2)}, u32[]{:S(2)}) %collective-permute-start.1) | collective-permute-done | bytes 1572896 | tf_op jit(solution)/shard_map/ppermute | solution.py:16
  237.7 2.2 fusion.132
  240.1 4.3 convolution_convert_fusion.1
  244.5 66.2 %all-gather.18.cloned.1.call-done = bf16[8,96,4096]{2,1,0:T(8,128)(2,1)} async-done(((bf16[2,96,4096]{2,1,0:T(8,128)(2,1)}), bf16[8,96,4096]{2,1,0:T(8,128)(2,1)}) %all-gather.18.cloned.1.call-update) | async-done | bytes 6291472 | tf_op jit(solution)/shard_map/all_gather | solution.py:164
  310.8 5.7 reduce_sum.700
  316.5 3.1 fusion.33
  319.6 2.1 collective-permute-start.2
  321.8 19.9 %collective-permute-done.2 = bf16[2,96,4096]{2,1,0:T(8,128)(2,1)} collective-permute-done((bf16[2,96,4096]{2,1,0:T(8,128)(2,1)}, bf16[2,96,4096]{2,1,0:T(8,128)(2,1)}, u32[]{:S(2)}, u32[]{:S(2)}) %collective-permute-start.2) | collective-permute-done | bytes 1572896 | tf_op jit(solution)/shard_map/ppermute | solution.py:16
  341.7 3.7 fusion.44
  346.2 2.5 copy-done.43
  355.4 2.2 fusion.133
  357.9 4.4 convolution_convert_fusion
  364.3 2.0 fusion.152
  366.3 62.3 %all-gather.20.cloned.1.call-done = bf16[8,96,4096]{2,1,0:T(8,128)(2,1)} async-done(((bf16[2,96,4096]{2,1,0:T(8,128)(2,1)}), bf16[8,96,4096]{2,1,0:T(8,128)(2,1)}) %all-gather.20.cloned.1.call-update) | async-done | bytes 6291472 | tf_op jit(solution)/shard_map/all_gather | solution.py:164
  428.6 5.6 reduce_sum.706
  434.2 4.7 fusion.68
  439.0 34.3 %all-gather.5 = bf16[8,2,4096]{2,1,0:T(2,128)(2,1)S(1)} all-gather(bf16[1,2,4096]{2,1,0:T(2,128)(2,1)S(1)} %fusion.387), channel_id=6, replica_groups=mesh['section'=4,'dp'=8,'mp'=4] {'dp'}, dimensions={0}, use_global_device_ids=true | all-gather | bytes 147456 | tf_op jit(solution)/shard_map/all_gather | solution.py:248
  486.6 2.2 fusion.105
  499.1 50.5 %all-reduce.34.cloned.1.call-done = bf16[2,96,4096]{2,1,0:T(8,128)(2,1)} async-done(((bf16[2,96,4096]{2,1,0:T(8,128)(2,1)}), bf16[2,96,4096]{2,1,0:T(8,128)(2,1)}) %all-reduce.34.cloned.1.call-update) | async-done | bytes 1572880 | tf_op jit(solution)/shard_map/psum | solution.py:200
  549.6 2.1 fusion.47
  553.5 2.1 collective-permute-start.3
  555.6 17.9 %collective-permute-done.3 = bf16[2,96,4096]{2,1,0:T(8,128)(2,1)S(1)} collective-permute-done((bf16[2,96,4096]{2,1,0:T(8,128)(2,1)S(1)}, bf16[2,96,4096]{2,1,0:T(8,128)(2,1)S(1)}, u32[]{:S(2)}, u32[]{:S(2)}) %collective-permute-start.3) | collective-permute-done | bytes 1572896 | tf_op jit(solution)/shard_map/ppermute | solution.py:16
  576.4 2.2 fusion.108
  589.5 51.8 %all-reduce.36.cloned.1.call-done = bf16[2,96,4096]{2,1,0:T(8,128)(2,1)} async-done(((bf16[2,96,4096]{2,1,0:T(8,128)(2,1)}), bf16[2,96,4096]{2,1,0:T(8,128)(2,1)}) %all-reduce.36.cloned.1.call-update) | async-done | bytes 1572880 | tf_op jit(solution)/shard_map/psum | solution.py:200
  641.3 2.2 fusion.48
  645.1 2.1 collective-permute-start.4
  647.2 17.7 %collective-permute-done.4 = bf16[2,96,4096]{2,1,0:T(8,128)(2,1)S(1)} collective-permute-done((bf16[2,96,4096]{2,1,0:T(8,128)(2,1)S(1)}, bf16[2,96,4096]{2,1,0:T(8,128)(2,1)S(1)}, u32[]{:S(2)}, u32[]{:S(2)}) %collective-permute-start.4) | collective-permute-done | bytes 1572896 | tf_op jit(solution)/shard_map/ppermute | solution.py:16
  667.9 2.3 fusion.111
  681.1 51.8 %all-reduce.38.cloned.1.call-done = bf16[2,96,4096]{2,1,0:T(8,128)(2,1)} async-done(((bf16[2,96,4096]{2,1,0:T(8,128)(2,1)}), bf16[2,96,4096]{2,1,0:T(8,128)(2,1)}) %all-reduce.38.cloned.1.call-update) | async-done | bytes 1572880 | tf_op jit(solution)/shard_map/psum | solution.py:200
  732.9 2.2 fusion.49
  736.8 2.3 collective-permute-start.5
  743.2 13.5 %collective-permute-done.5 = bf16[2,96,4096]{2,1,0:T(8,128)(2,1)S(1)} collective-permute-done((bf16[2,96,4096]{2,1,0:T(8,128)(2,1)S(1)}, bf16[2,96,4096]{2,1,0:T(8,128)(2,1)S(1)}, u32[]{:S(2)}, u32[]{:S(2)}) %collective-permute-start.5) | collective-permute-done | bytes 1572896 | tf_op jit(solution)/shard_map/ppermute | solution.py:16
  758.5 2.2 fusion.114
  766.7 2.1 copy.221
  770.5 6.5 all-to-all-start.2
  777.3 4.4 copy.230
  790.2 1.9 fusion.57
  792.1 7.6 all-to-all-start.1
  800.3 2.4 copy.227
  802.7 6.9 fusion.66
  810.7 7.6 all-to-all-start
  818.4 2.4 fusion.658
  820.8 7.3 all-to-all-done
  828.1 19.9 %all_to_all.26 = bf16[8,96,512]{2,1,0:T(8,128)(2,1)} all-to-all(bf16[8,96,512]{2,1,0:T(8,128)(2,1)S(1)} %get-tuple-element.62), channel_id=1, replica_groups=mesh['section'=4,'dp'=8,'mp'=4] {'dp'}, dimensions={0} | all-to-all | bytes 1572864 | tf_op jit(solution)/shard_map/all_to_all | solution.py:47
  848.0 4.9 all-to-all-start.3
  859.9 4.1 all-to-all-done.3
  864.0 2.6 pad_maximum_fusion.1
  866.6 3.2 fusion.61
  871.8 3.4 fusion.97
  (485 shorter events, 105.1 us)
Async XLA Ops:
  7.2 14.1 %copy-start = (bf16[1,4096,128]{2,1,0:T(8,128)(2,1)S(1)}, bf16[1,4096,128]{2,1,0:T(8,128)(2,1)}, u32[]{:S(2)}) copy-start(bf16[1,4096,128]{2,1,0:T(8,128)(2,1)} %param.14) | copy-start | bytes 3145732
  7.2 87.3 %all-gather.14.cloned.1.call-start = ((), (), s32[]{:S(2)}) async-start(), calls=%async_computation.9 | async-start | bytes 7864320 | tf_op jit(solution)/shard_map/all_gather | solution.py:164
  7.3 356.6 %copy-start.70 = (pred[96,96]{0,1:T(8,128)(4,1)}, pred[96,96]{0,1:T(8,128)(4,1)S(1)}, u32[]{:S(2)}) copy-start(pred[96,96]{0,1:T(8,128)(4,1)S(1)} %iota_compare_fusion) | copy-start | bytes 27652
  9.2 6.8 copy-start.9
  9.2 6.8 copy-start.58
  26.6 177.1 %all-gather.16.cloned.1.call-start = ((), (), s32[]{:S(2)}) async-start(), calls=%async_computation.10 | async-start | bytes 7864320 | tf_op jit(solution)/shard_map/all_gather | solution.py:164
  103.2 22.0 %collective-permute-start = (bf16[2,96,4096]{2,1,0:T(8,128)(2,1)}, bf16[2,96,4096]{2,1,0:T(8,128)(2,1)}, u32[]{:S(2)}, u32[]{:S(2)}) collective-permute-start(bf16[2,96,4096]{2,1,0:T(8,128)(2,1)} %fusion.25), channel_id=1, source_target_pairs={{0,32},{32,64},{64,96},{1,33},{33,65},{65,97},{2,34},{34,66},{66,9... | collective-permute-start | bytes 4718600 | tf_op jit(solution)/shard_map/ppermute | solution.py:16
  105.6 21.7 %copy-start.41 = (bf16[512,4096]{1,0:T(8,128)(2,1)S(1)}, bf16[512,4096]{1,0:T(8,128)(2,1)}, u32[]{:S(2)}) copy-start(bf16[512,4096]{1,0:T(8,128)(2,1)} %copy.215) | copy-start | bytes 12582916
  137.4 173.4 %all-gather.18.cloned.1.call-start = ((), (), s32[]{:S(2)}) async-start(), calls=%async_computation.11 | async-start | bytes 7864320 | tf_op jit(solution)/shard_map/all_gather | solution.py:164
  211.7 22.8 %copy-start.54 = (bf16[2,96,4096]{2,1,0:T(8,128)(2,1)}, bf16[2,96,4096]{2,1,0:T(8,128)(2,1)S(1)}, u32[]{:S(2)}) copy-start(bf16[2,96,4096]{2,1,0:T(8,128)(2,1)S(1)} %fusion.29) | copy-start | bytes 4718596
  211.7 22.8 %copy-start.42 = (bf16[512,4096]{1,0:T(8,128)(2,1)S(1)}, bf16[512,4096]{1,0:T(8,128)(2,1)}, u32[]{:S(2)}) copy-start(bf16[512,4096]{1,0:T(8,128)(2,1)} %copy.215) | copy-start | bytes 12582916
  211.7 22.0 %collective-permute-start.1 = (bf16[2,96,4096]{2,1,0:T(8,128)(2,1)S(1)}, bf16[2,96,4096]{2,1,0:T(8,128)(2,1)S(1)}, u32[]{:S(2)}, u32[]{:S(2)}) collective-permute-start(bf16[2,96,4096]{2,1,0:T(8,128)(2,1)S(1)} %fusion.29), channel_id=1, source_target_pairs={{0,32},{32,64},{64,96},{1,33},{33,65},{65,97},{2,34},{34,66},{66,9... | collective-permute-start | bytes 4718600 | tf_op jit(solution)/shard_map/ppermute | solution.py:16
  244.5 184.1 %all-gather.20.cloned.1.call-start = ((), (), s32[]{:S(2)}) async-start(), calls=%async_computation.12 | async-start | bytes 7864320 | tf_op jit(solution)/shard_map/all_gather | solution.py:164
  310.8 5.7 copy-start.24
  319.6 22.0 %collective-permute-start.2 = (bf16[2,96,4096]{2,1,0:T(8,128)(2,1)}, bf16[2,96,4096]{2,1,0:T(8,128)(2,1)}, u32[]{:S(2)}, u32[]{:S(2)}) collective-permute-start(bf16[2,96,4096]{2,1,0:T(8,128)(2,1)} %fusion.33), channel_id=1, source_target_pairs={{0,32},{32,64},{64,96},{1,33},{33,65},{65,97},{2,34},{34,66},{66,9... | collective-permute-start | bytes 4718600 | tf_op jit(solution)/shard_map/ppermute | solution.py:16
  345.3 4.9 copy-start.118
  345.4 7.1 copy-start.40
  345.4 4.8 copy-start.107
  346.2 4.0 copy-start.18
  357.8 5.0 copy-start.122
  357.8 5.8 copy-start.96
  357.8 5.8 copy-start.97
  357.8 5.9 copy-start.62
  357.9 5.9 copy-start.63
  362.3 187.3 %all-reduce.34.cloned.1.call-start = ((), (), s32[]{:S(2)}) async-start(), calls=%async_computation.5 | async-start | bytes 3145728 | tf_op jit(solution)/shard_map/psum | solution.py:200
  363.0 75.9 %copy-start.120 = (f32[2]{0:T(128)}, f32[2]{0:T(128)S(1)}, u32[]{:S(2)}) copy-start(f32[2]{0:T(128)S(1)} %fusion.646) | copy-start | bytes 28
  363.9 128.3 %copy-start.64 = (bf16[2,96,4,128]{3,1,2,0:T(8,128)(2,1)}, bf16[2,96,4,128]{3,1,2,0:T(8,128)(2,1)S(1)}, u32[]{:S(2)}) copy-start(bf16[2,96,4,128]{3,1,2,0:T(8,128)(2,1)S(1)} %pad_maximum_fusion.3) | copy-start | bytes 589828
  364.2 128.0 %copy-start.98 = (f32[2,4,96]{2,1,0:T(4,128)}, f32[2,4,96]{2,1,0:T(4,128)S(1)}, u32[]{:S(2)}) copy-start(f32[2,4,96]{2,1,0:T(4,128)S(1)} %get-tuple-element.182) | copy-start | bytes 9220
  364.3 69.9 %copy-start.113 = (f32[2,4,96]{2,1,0:T(4,128)}, f32[2,4,96]{2,1,0:T(4,128)S(1)}, u32[]{:S(2)}) copy-start(f32[2,4,96]{2,1,0:T(4,128)S(1)} %fusion.647) | copy-start | bytes 9220
  364.3 126.2 %copy-start.100 = (f32[2,4,96]{2,1,0:T(4,128)}, f32[2,4,96]{2,1,0:T(4,128)S(1)}, u32[]{:S(2)}) copy-start(f32[2,4,96]{2,1,0:T(4,128)S(1)} %multiply_divide_fusion) | copy-start | bytes 9220
  366.3 124.2 %copy-start.55 = (bf16[2,96,128,1]{2,1,3,0:T(8,128)(2,1)}, bf16[2,96,128,1]{2,1,3,0:T(8,128)(2,1)S(1)}, u32[]{:S(2)}) copy-start(bf16[2,96,128,1]{2,1,3,0:T(8,128)(2,1)S(1)} %fusion.152) | copy-start | bytes 147460
  434.2 42.4 %copy-start.112 = (s32[8]{0:T(128)S(1)}, s32[8]{0:T(128)}, u32[]{:S(2)}) copy-start(s32[8]{0:T(128)} %param.10) | copy-start | bytes 100
  473.3 13.2 %copy-start.121 = (f32[2]{0:T(128)S(1)}, f32[2]{0:T(128)}, u32[]{:S(2)}) copy-start(f32[2]{0:T(128)} %copy-done.120) | copy-start | bytes 28
  473.3 13.3 %copy-start.5 = (bf16[1,512,4096]{2,1,0:T(8,128)(2,1)S(1)}, bf16[1,512,4096]{2,1,0:T(8,128)(2,1)}, u32[]{:S(2)}) copy-start(bf16[1,512,4096]{2,1,0:T(8,128)(2,1)} %param.15) | copy-start | bytes 12582916
  473.3 13.3 %copy-start.102 = (f32[2,96]{1,0:T(2,128)S(1)}, f32[2,96]{1,0:T(2,128)}, u32[]{:S(2)}) copy-start(f32[2,96]{1,0:T(2,128)} %get-tuple-element.123) | copy-start | bytes 2308
  486.6 5.2 copy-start.71
  486.6 5.2 copy-start.94
  493.0 4.1 copy-start.79
  498.9 142.4 %all-reduce.36.cloned.1.call-start = ((), (), s32[]{:S(2)}) async-start(), calls=%async_computation.6 | async-start | bytes 3145728 | tf_op jit(solution)/shard_map/psum | solution.py:200
  552.3 24.1 %copy-start.6 = (bf16[1,512,4096]{2,1,0:T(8,128)(2,1)S(1)}, bf16[1,512,4096]{2,1,0:T(8,128)(2,1)}, u32[]{:S(2)}) copy-start(bf16[1,512,4096]{2,1,0:T(8,128)(2,1)} %param.15) | copy-start | bytes 12582916
  553.5 20.0 %collective-permute-start.3 = (bf16[2,96,4096]{2,1,0:T(8,128)(2,1)S(1)}, bf16[2,96,4096]{2,1,0:T(8,128)(2,1)S(1)}, u32[]{:S(2)}, u32[]{:S(2)}) collective-permute-start(bf16[2,96,4096]{2,1,0:T(8,128)(2,1)S(1)} %fusion.42), channel_id=1, source_target_pairs={{32,0},{64,32},{96,64},{33,1},{65,33},{97,65},{34,2},{66,34},{98,6... | collective-permute-start | bytes 4718600 | tf_op jit(solution)/shard_map/ppermute | solution.py:16
  589.5 143.5 %all-reduce.38.cloned.1.call-start = ((), (), s32[]{:S(2)}) async-start(), calls=%async_computation.7 | async-start | bytes 3145728 | tf_op jit(solution)/shard_map/psum | solution.py:200
  643.7 24.2 %copy-start.7 = (bf16[1,512,4096]{2,1,0:T(8,128)(2,1)S(1)}, bf16[1,512,4096]{2,1,0:T(8,128)(2,1)}, u32[]{:S(2)}) copy-start(bf16[1,512,4096]{2,1,0:T(8,128)(2,1)} %param.15) | copy-start | bytes 12582916
  645.1 19.8 %collective-permute-start.4 = (bf16[2,96,4096]{2,1,0:T(8,128)(2,1)S(1)}, bf16[2,96,4096]{2,1,0:T(8,128)(2,1)S(1)}, u32[]{:S(2)}, u32[]{:S(2)}) collective-permute-start(bf16[2,96,4096]{2,1,0:T(8,128)(2,1)S(1)} %fusion.39), channel_id=1, source_target_pairs={{32,0},{64,32},{96,64},{33,1},{65,33},{97,65},{34,2},{66,34},{98,6... | collective-permute-start | bytes 4718600 | tf_op jit(solution)/shard_map/ppermute | solution.py:16
  681.1 185.6 %all-gather.12.cloned.1.call-start = ((), (), s32[]{:S(2)}) async-start(), calls=%async_computation.8 | async-start | bytes 4423680 | tf_op jit(solution)/shard_map/all_gather | solution.py:57
  735.3 4.9 copy-start.45
  735.3 5.9 copy-start.47
  735.3 5.9 copy-start.49
  736.7 5.5 copy-start.51
  736.7 5.4 copy-start.53
  736.8 20.0 %collective-permute-start.5 = (bf16[2,96,4096]{2,1,0:T(8,128)(2,1)S(1)}, bf16[2,96,4096]{2,1,0:T(8,128)(2,1)S(1)}, u32[]{:S(2)}, u32[]{:S(2)}) collective-permute-start(bf16[2,96,4096]{2,1,0:T(8,128)(2,1)S(1)} %fusion.41), channel_id=1, source_target_pairs={{32,0},{64,32},{96,64},{33,1},{65,33},{97,65},{34,2},{66,34},{98,6... | collective-permute-start | bytes 4718600 | tf_op jit(solution)/shard_map/ppermute | solution.py:16
  741.2 17.2 %copy-start.8 = (bf16[1,512,4096]{2,1,0:T(8,128)(2,1)S(1)}, bf16[1,512,4096]{2,1,0:T(8,128)(2,1)}, u32[]{:S(2)}) copy-start(bf16[1,512,4096]{2,1,0:T(8,128)(2,1)} %param.15) | copy-start | bytes 12582916
  758.4 4.0 copy-start.99
  758.4 4.0 copy-start.101
  758.4 5.3 copy-start.72
  758.4 5.3 copy-start.95
  758.4 5.3 copy-start.115
  770.5 21.6 %all-to-all-start.2 = ((bf16[8,96,512]{2,1,0:T(8,128)(2,1)}), bf16[8,96,512]{2,1,0:T(8,128)(2,1)}, u32[]{:S(2)}, u32[]{:S(2)}) async-start(bf16[8,96,512]{2,1,0:T(8,128)(2,1)} %get-tuple-element.66), calls=%async_computation.2 | async-start | bytes 1572864 | tf_op jit(solution)/shard_map/all_to_all | solution.py:47
  777.3 4.4 copy-start.27
  792.1 10.6 %copy-start.39 = (bf16[24,8,8,512]{3,2,1,0:T(8,128)(2,1)S(1)}, bf16[24,8,8,512]{3,2,1,0:T(8,128)(2,1)}, u32[]{:S(2)}) copy-start(bf16[24,8,8,512]{3,2,1,0:T(8,128)(2,1)} %copy.229) | copy-start | bytes 4718596
  792.1 18.6 %all-to-all-start.1 = ((bf16[8,96,512]{2,1,0:T(8,128)(2,1)}), bf16[8,96,512]{2,1,0:T(8,128)(2,1)S(1)}, u32[]{:S(2)}, u32[]{:S(2)}) async-start(bf16[8,96,512]{2,1,0:T(8,128)(2,1)} %get-tuple-element.65), calls=%async_computation.1 | async-start | bytes 1572864 | tf_op jit(solution)/shard_map/all_to_all | solution.py:47
  810.7 17.4 %all-to-all-start = ((f32[32,1,128]{2,1,0:T(1,128)}), f32[32,1,128]{2,1,0:T(1,128)S(1)}, u32[]{:S(2)}, u32[]{:S(2)}) async-start(f32[32,1,128]{2,1,0:T(1,128)} %bitcast.217), calls=%async_computation | async-start | bytes 32768 | tf_op jit(solution)/shard_map/all_to_all | solution.py:26
  848.0 16.0 %all-to-all-start.3 = ((bf16[8,96,512]{2,1,0:T(8,128)(2,1)}), bf16[8,96,512]{2,1,0:T(8,128)(2,1)}, u32[]{:S(2)}, u32[]{:S(2)}) async-start(bf16[8,96,512]{2,1,0:T(8,128)(2,1)} %get-tuple-element.61), calls=%async_computation.3 | async-start | bytes 1572864 | tf_op jit(solution)/shard_map/all_to_all | solution.py:47
  866.6 5.1 copy-start.38
  (77 other events, 165.5 us)
Sparse Core Ops, SparseCore 0:
  26.7 67.7 all-gather.13
  137.5 66.1 all-gather.15
  244.6 66.1 all-gather.17
  362.4 66.1 all-gather.19
  499.0 50.5 all-reduce.33
  589.6 51.6 all-reduce.35
  681.2 51.6 all-reduce.37
  766.7 83.9 all-gather.11
